TPU v7x, 512 devices: a whole 4x4x16 slice. The times are simulated.
512 devices in a mesh: ctx: 16 (over x, z_hi), fsdp: 32 (over z_lo, y, core).
Axes of the slice: x: 4, y: 4, z: 16 (z_hi: 4, z_lo: 4; z = z_hi * 4 + z_lo), core: 2. Of those that a mesh axis runs over, the one named last changes fastest.
Arguments:
- block_pos: int32 [8, 16], P(None, 'ctx'), may hold values from 0 to 15, each once within a row
- queries: bfloat16 [32, 2048, 640], P('fsdp', 'ctx'), may hold values from -6 to 6
- keys: bfloat16 [32, 2048, 128], P('fsdp', 'ctx'), may hold values from -6 to 6
- values: bfloat16 [32, 2048, 128], P('fsdp', 'ctx'), may hold values from -12 to 12
- attention_output: bfloat16 [32, 2048, 640], P('fsdp', 'ctx'), may hold values from -6 to 6
- output_gradient: bfloat16 [32, 2048, 640], P('fsdp', 'ctx'), may hold values from -24 to 24
- log_softmax_norm: float32 [32, 5, 2048], P('fsdp', None, 'ctx'), may hold values from 6 to 9
- features: bfloat16 [8, 2048, 2560], P(None, 'ctx', 'fsdp'), may hold values from -0.119628906 to 0.119628906
Outputs:
- grad_q: bfloat16 [32, 2048, 640], P('fsdp', 'ctx')
- key_gradient: bfloat16 [32, 2048, 128], P('fsdp', 'ctx')
- value_gradient: bfloat16 [32, 2048, 128], P('fsdp', 'ctx')
- grad_wk: float32 [2560, 512], P('fsdp')
Inputs may be any that keep to these rules, and one draw needn't show every extreme that they name: Each row of block_pos holds every block place 0 to 15 once.
All inputs are finite; a program needn't handle non-finite values.
Results may differ from a plain program's by a relative error of at most 0.0058.
Values may be sent and summed in bfloat16 or wider, within the bound.
No kernel may reach another device: no remote copies, remote signals or barrier semaphores. Data moves between devices by JAX's collectives and lax.ppermute only.
A program may use at most 64 MiB of HBM per device.

v0:
```python
import jax
import jax.numpy as jnp
from jax import lax
from jax.sharding import PartitionSpec as P

QUERY_HEADS = 20
KEY_VALUE_HEADS = 4
HEAD_SIZE = 128
HEAD_GROUPS = 4


def from_behind(value, axis, steps):
    count = lax.axis_size(axis)
    pairs = [(source, (source + steps) % count) for source in range(count)]
    return lax.ppermute(value, axis, pairs)


def shortened(shard):

    def short(part):
        return part.astype(jnp.bfloat16) if part.dtype == jnp.float32 else part

    return jax.tree.map(short, shard)


def block_grads(
    heads_of_queries,
    head_gradient,
    delta_heads,
    heads_of_norm,
    block_of_keys,
    block_of_values,
    key_place,
    key_offset,
    own_place,
):
    query_rows = heads_of_queries.shape[0]
    key_rows = block_of_keys.shape[0]
    score_scale = heads_of_queries.shape[-1] ** (-0.5)
    query_pos = own_place * query_rows + lax.iota(jnp.int32, query_rows)
    key_pos = key_place[0] * query_rows + key_offset + lax.iota(jnp.int32, key_rows)
    visible = key_pos[None, :] <= query_pos[:, None]
    scores = (
        jnp.einsum(
            "tkgd,ukd->kgtu", heads_of_queries, block_of_keys, preferred_element_type=jnp.float32
        )
        * score_scale
    )
    soft_probs = jnp.where(visible, jnp.exp(scores - heads_of_norm[..., None]), 0.0)
    dprobs = jnp.einsum(
        "tkgd,ukd->kgtu", head_gradient, block_of_values, preferred_element_type=jnp.float32
    )
    dscores = (soft_probs * (dprobs - delta_heads[..., None]) * score_scale).astype(jnp.bfloat16)
    probs_low = soft_probs.astype(jnp.bfloat16)
    grad_query = jnp.einsum(
        "kgtu,ukd->tkgd", dscores, block_of_keys, preferred_element_type=jnp.float32
    )
    gradient_for_key = jnp.einsum(
        "kgtu,tkgd->ukd", dscores, heads_of_queries, preferred_element_type=jnp.float32
    )
    gradient_for_value = jnp.einsum(
        "kgtu,tkgd->ukd", probs_low, head_gradient, preferred_element_type=jnp.float32
    )
    return (grad_query, gradient_for_key, gradient_for_value)


def local(
    block_pos, queries, keys, values, attention_output, output_gradient, log_softmax_norm, features
):
    rows_per_block = queries.shape[1]
    group_size = QUERY_HEADS // KEY_VALUE_HEADS
    kv_local = keys.shape[-1] // HEAD_SIZE
    sequence_index = lax.axis_index("fsdp") // HEAD_GROUPS
    own_row = lax.dynamic_slice_in_dim(block_pos, sequence_index, 1, 0)
    own_place = own_row[0, 0]
    key_place = own_row[0, 0:1]
    heads_of_queries = queries[0].reshape(rows_per_block, kv_local, group_size, HEAD_SIZE)
    head_gradient = output_gradient[0].reshape(rows_per_block, kv_local, group_size, HEAD_SIZE)
    heads_of_output = attention_output[0].reshape(rows_per_block, kv_local, group_size, HEAD_SIZE)
    delta = jnp.sum(
        head_gradient.astype(jnp.float32) * heads_of_output.astype(jnp.float32), axis=-1
    )
    delta_heads = jnp.transpose(delta, (1, 2, 0))
    heads_of_norm = log_softmax_norm[0].reshape(kv_local, group_size, rows_per_block)
    block_of_keys = keys[0].reshape(rows_per_block, kv_local, HEAD_SIZE)
    block_of_values = values[0].reshape(rows_per_block, kv_local, HEAD_SIZE)
    cycle_length = lax.axis_size("ctx")
    zero_key_gradient = jnp.zeros((rows_per_block, kv_local, HEAD_SIZE), jnp.float32)
    zero_query_gradient = jnp.zeros((rows_per_block, kv_local, group_size, HEAD_SIZE), jnp.float32)

    def visit_rows(query_acc, blocks, grad_pair, key_offset):
        add_query, add_key, add_value = block_grads(
            heads_of_queries,
            head_gradient,
            delta_heads,
            heads_of_norm,
            blocks[0],
            blocks[1],
            blocks[2],
            key_offset,
            own_place,
        )
        return (query_acc + add_query, (grad_pair[0] + add_key, grad_pair[1] + add_value))

    def visit(query_acc, blocks, grad_pair):
        return visit_rows(query_acc, blocks, grad_pair, 0)

    def pass_grads(grad_pair):
        return from_behind(grad_pair, "ctx", 1)

    def cycle_step(step_index, cycle_state):
        query_acc, blocks, grad_pair = cycle_state
        query_acc, grad_pair = visit(query_acc, blocks, grad_pair)
        blocks = jax.tree.map(
            lambda part, own: part.astype(own.dtype),
            from_behind(shortened(blocks), "ctx", 1),
            blocks,
        )
        grad_pair = pass_grads(grad_pair)
        return (query_acc, blocks, grad_pair)

    cycle_state = (
        zero_query_gradient,
        (block_of_keys, block_of_values, key_place),
        (zero_key_gradient, zero_key_gradient),
    )
    query_acc, blocks, grad_pair = lax.fori_loop(0, cycle_length - 1, cycle_step, cycle_state)
    query_acc, grad_pair = visit(query_acc, blocks, grad_pair)
    grad_pair = pass_grads(grad_pair)
    key_gradient_sum = grad_pair[0]
    value_gradient_sum = grad_pair[1]
    grad_q = query_acc.reshape(rows_per_block, -1).astype(jnp.bfloat16)
    key_gradient = key_gradient_sum.reshape(rows_per_block, -1).astype(jnp.bfloat16)
    value_gradient = value_gradient_sum.reshape(rows_per_block, -1).astype(jnp.bfloat16)
    local_width = key_gradient.shape[-1]
    feature_cols = features.shape[-1]
    piece = lax.all_gather(key_gradient[None], "fsdp", axis=0, tiled=True)
    count = piece.shape[0]
    indices = lax.iota(jnp.int32, count)
    seq_ids = indices // HEAD_GROUPS
    group_ids = indices % HEAD_GROUPS
    chosen = jnp.take(features, seq_ids, axis=0)
    contrib = jnp.einsum("pti,ptj->pij", chosen, piece, preferred_element_type=jnp.float32)
    rounded = lax.optimization_barrier(contrib.astype(jnp.bfloat16)).astype(jnp.float32)
    placing = (group_ids[:, None] == lax.iota(jnp.int32, HEAD_GROUPS)[None, :]).astype(jnp.float32)
    summed = jnp.einsum("pij,pr->irj", rounded, placing)
    summed = summed.reshape(feature_cols, HEAD_GROUPS * local_width)
    grad_wk = lax.psum(summed, "ctx")
    return (grad_q[None], key_gradient[None], value_gradient[None], grad_wk)


def solution(mesh):
    return jax.shard_map(
        local,
        mesh=mesh,
        in_specs=(
            P(None, "ctx"),
            P("fsdp", "ctx", None),
            P("fsdp", "ctx", None),
            P("fsdp", "ctx", None),
            P("fsdp", "ctx", None),
            P("fsdp", "ctx", None),
            P("fsdp", None, "ctx"),
            P(None, "ctx", "fsdp"),
        ),
        out_specs=(
            P("fsdp", "ctx", None),
            P("fsdp", "ctx", None),
            P("fsdp", "ctx", None),
            P("fsdp", None),
        ),
        check_vma=False,
    )
```

profile of v0, /device:TPU:2, one launch (start us, length us, event | category | flops | bytes accessed | tf_op | source)
XLA Modules:
  0.0 845.0 jit_solution(10300200507523520744)
XLA Ops:
  12.6 541.2 %while.23 = (s32[]{:T(128)}, f32[128,1,5,128]{3,0,2,1:T(8,128)S(1)}, bf16[128,1,128]{2,0,1:T(8,128)(2,1)S(1)}, bf16[128,1,128]{2,0,1:T(8,128)(2,1)S(1)}, s32[1]{...) while((s32[]{:T(128)}, ...), condition=%wide.region_2.3_spmd.clone, body=%wide.region_1.2_spmd.clone.sunk | while | flops 105726208 | bytes 4103563 | solution.py:127
  12.6 9.1 %collective-permute-start = (bf16[128,1,128]{2,0,1:T(8,128)(2,1)S(1)}, bf16[128,1,128]{2,0,1:T(8,128)(2,1)S(1)}, u32[]{:S(2)}, u32[]{:S(2)}) collective-permute-start(bf16[128,1,128]{2,0,1:T(8,128)(2,1)S(1)} %copy.66), channel_id=1, source_target_pairs={{0,32},{32,64},{64,96},{96,128},{128,160},{160,192},{192,224},{224... | collective-permute-start | bytes 98312 | tf_op jit(solution)/shard_map/while/body/eval_jaxpr/ppermute | solution.py:15
  21.7 9.1 %collective-permute-start.1 = (bf16[128,1,128]{2,0,1:T(8,128)(2,1)S(1)}, bf16[128,1,128]{2,0,1:T(8,128)(2,1)S(1)}, u32[]{:S(2)}, u32[]{:S(2)}) collective-permute-start(bf16[128,1,128]{2,0,1:T(8,128)(2,1)S(1)} %copy.67), channel_id=1, source_target_pairs={{0,32},{32,64},{64,96},{96,128},{128,160},{160,192},{192,224},{224... | collective-permute-start | bytes 98312 | tf_op jit(solution)/shard_map/while/body/eval_jaxpr/ppermute | solution.py:15
  31.4 5.6 collective-permute-start.2
  45.9 7.4 collective-permute-done.3
  57.8 8.3 collective-permute-start.1
  94.6 8.3 collective-permute-start.1
  119.1 6.7 collective-permute-done.4
  125.8 8.3 collective-permute-start
  148.5 7.0 collective-permute-start.4
  160.6 6.0 collective-permute-start
  166.6 6.5 collective-permute-start.1
  180.2 6.9 collective-permute-start.3
  192.3 5.9 collective-permute-done.4
  201.6 6.5 collective-permute-start.1
  208.6 7.9 collective-permute-start.2
  236.2 6.1 collective-permute-start.1
  247.4 7.0 collective-permute-start.3
  254.6 8.1 collective-permute-start.4
  266.0 6.8 collective-permute-start
  272.8 5.9 collective-permute-start.1
  284.9 6.5 collective-permute-start.3
  291.6 5.5 collective-permute-start.4
  297.5 7.8 collective-permute-done.4
  308.2 8.9 %collective-permute-start.1 = (bf16[128,1,128]{2,0,1:T(8,128)(2,1)S(1)}, bf16[128,1,128]{2,0,1:T(8,128)(2,1)S(1)}, u32[]{:S(2)}, u32[]{:S(2)}) collective-permute-start(bf16[128,1,128]{2,0,1:T(8,128)(2,1)S(1)} %copy.67), channel_id=1, source_target_pairs={{0,32},{32,64},{64,96},{96,128},{128,160},{160,192},{192,224},{224... | collective-permute-start | bytes 98312 | tf_op jit(solution)/shard_map/while/body/eval_jaxpr/ppermute | solution.py:15
  322.3 6.0 collective-permute-start.3
  333.6 6.4 collective-permute-done.4
  341.9 7.4 collective-permute-start.1
  349.8 9.7 %collective-permute-start.2 = (s32[1]{0:T(128)}, s32[1]{0:T(128)}, u32[]{:S(2)}, u32[]{:S(2)}) collective-permute-start(s32[1]{0:T(128)} %copy.68), channel_id=1, source_target_pairs={{0,32},{32,64},{64,96},{96,128},{128,160},{160,192},{192,224},{224... | collective-permute-start | bytes 20 | tf_op jit(solution)/shard_map/while/body/eval_jaxpr/ppermute | solution.py:15
  367.1 6.4 collective-permute-done.3
  384.5 7.4 collective-permute-start.2
  398.7 6.0 collective-permute-start.4
  405.2 5.6 collective-permute-done.4
  415.0 7.3 collective-permute-start.1
  422.8 6.1 collective-permute-start.2
  435.3 6.0 collective-permute-start.4
  446.3 6.5 collective-permute-start
  452.8 6.1 collective-permute-start.1
  465.1 5.7 collective-permute-start.3
  476.0 6.7 collective-permute-done.4
  490.0 9.6 %collective-permute-start.2 = (s32[1]{0:T(128)}, s32[1]{0:T(128)}, u32[]{:S(2)}, u32[]{:S(2)}) collective-permute-start(s32[1]{0:T(128)} %copy.68), channel_id=1, source_target_pairs={{0,32},{32,64},{64,96},{96,128},{128,160},{160,192},{192,224},{224... | collective-permute-start | bytes 20 | tf_op jit(solution)/shard_map/while/body/eval_jaxpr/ppermute | solution.py:15
  512.0 6.8 collective-permute-done.4
  523.2 8.2 collective-permute-start.2
  532.8 9.4 %collective-permute-start.3 = (f32[128,1,128]{2,0,1:T(8,128)S(1)}, f32[128,1,128]{2,0,1:T(8,128)S(1)}, u32[]{:S(2)}, u32[]{:S(2)}) collective-permute-start(f32[128,1,128]{2,0,1:T(8,128)S(1)} %fusion.89), channel_id=1, source_target_pairs={{0,32},{32,64},{64,96},{96,128},{128,160},{160,192},{192,224},{224... | collective-permute-start | bytes 196616 | tf_op jit(solution)/shard_map/while/body/eval_jaxpr/ppermute | solution.py:15
  544.7 9.1 %collective-permute-done.4 = f32[128,1,128]{2,0,1:T(8,128)S(1)} collective-permute-done((f32[128,1,128]{2,0,1:T(8,128)S(1)}, f32[128,1,128]{2,0,1:T(8,128)S(1)}, u32[]{:S(2)}, u32[]{:S(2)}) %collective-permute-start.4) | collective-permute-done | bytes 65568 | tf_op jit(solution)/shard_map/while/body/eval_jaxpr/ppermute | solution.py:15
  557.7 8.7 %collective-permute-done.5 = bf16[128,1,128]{2,0,1:T(8,128)(2,1)S(1)} collective-permute-done((bf16[128,1,128]{2,0,1:T(8,128)(2,1)S(1)}, bf16[128,1,128]{2,0,1:T(8,128)(2,1)S(1)}, u32[]{:S(2)}, u32[]{:S(2)}) %collective-permute-start.5) | collective-permute-done | bytes 32800 | tf_op jit(solution)/shard_map/ppermute | solution.py:15
  570.1 63.8 %all-gather.3.cloned.1.call-done = bf16[4096,1,128]{2,0,1:T(8,128)(2,1)} async-done(((bf16[128,1,128]{2,0,1:T(8,128)(2,1)}), bf16[4096,1,128]{2,0,1:T(8,128)(2,1)}) %all-gather.3.cloned.1.call-update) | async-done | bytes 1048592 | tf_op jit(solution)/shard_map/all_gather | solution.py:137
  637.8 197.5 %all-reduce.2.cloned.1.call-done = f32[80,512]{1,0:T(8,128)} async-done(((f32[80,512]{1,0:T(8,128)}), f32[80,512]{1,0:T(8,128)}) %all-reduce.2.cloned.1.call-update) | async-done | bytes 163856 | tf_op jit(solution)/shard_map/psum | solution.py:148
  (315 shorter events, 235.7 us)
Async XLA Ops:
  7.2 626.7 %all-gather.3.cloned.1.call-start = ((), (), s32[]{:S(2)}) async-start(), calls=%async_computation.1 | async-start | bytes 1081344 | tf_op jit(solution)/shard_map/all_gather | solution.py:137
  12.6 33.3 %collective-permute-start = (bf16[128,1,128]{2,0,1:T(8,128)(2,1)S(1)}, bf16[128,1,128]{2,0,1:T(8,128)(2,1)S(1)}, u32[]{:S(2)}, u32[]{:S(2)}) collective-permute-start(bf16[128,1,128]{2,0,1:T(8,128)(2,1)S(1)} %copy.66), channel_id=1, source_target_pairs={{0,32},{32,64},{64,96},{96,128},{128,160},{160,192},{192,224},{224... | collective-permute-start | bytes 98312 | tf_op jit(solution)/shard_map/while/body/eval_jaxpr/ppermute | solution.py:15
  21.7 24.2 %collective-permute-start.1 = (bf16[128,1,128]{2,0,1:T(8,128)(2,1)S(1)}, bf16[128,1,128]{2,0,1:T(8,128)(2,1)S(1)}, u32[]{:S(2)}, u32[]{:S(2)}) collective-permute-start(bf16[128,1,128]{2,0,1:T(8,128)(2,1)S(1)} %copy.67), channel_id=1, source_target_pairs={{0,32},{32,64},{64,96},{96,128},{128,160},{160,192},{192,224},{224... | collective-permute-start | bytes 98312 | tf_op jit(solution)/shard_map/while/body/eval_jaxpr/ppermute | solution.py:15
  31.4 14.5 %collective-permute-start.2 = (s32[1]{0:T(128)}, s32[1]{0:T(128)}, u32[]{:S(2)}, u32[]{:S(2)}) collective-permute-start(s32[1]{0:T(128)} %copy.68), channel_id=1, source_target_pairs={{0,32},{32,64},{64,96},{96,128},{128,160},{160,192},{192,224},{224... | collective-permute-start | bytes 20 | tf_op jit(solution)/shard_map/while/body/eval_jaxpr/ppermute | solution.py:15
  38.3 15.0 %collective-permute-start.3 = (f32[128,1,128]{2,0,1:T(8,128)S(1)}, f32[128,1,128]{2,0,1:T(8,128)S(1)}, u32[]{:S(2)}, u32[]{:S(2)}) collective-permute-start(f32[128,1,128]{2,0,1:T(8,128)S(1)} %fusion.89), channel_id=1, source_target_pairs={{0,32},{32,64},{64,96},{96,128},{128,160},{160,192},{192,224},{224... | collective-permute-start | bytes 196616 | tf_op jit(solution)/shard_map/while/body/eval_jaxpr/ppermute | solution.py:15
  54.0 27.8 %collective-permute-start = (bf16[128,1,128]{2,0,1:T(8,128)(2,1)S(1)}, bf16[128,1,128]{2,0,1:T(8,128)(2,1)S(1)}, u32[]{:S(2)}, u32[]{:S(2)}) collective-permute-start(bf16[128,1,128]{2,0,1:T(8,128)(2,1)S(1)} %copy.66), channel_id=1, source_target_pairs={{0,32},{32,64},{64,96},{96,128},{128,160},{160,192},{192,224},{224... | collective-permute-start | bytes 98312 | tf_op jit(solution)/shard_map/while/body/eval_jaxpr/ppermute | solution.py:15
  57.8 24.0 %collective-permute-start.1 = (bf16[128,1,128]{2,0,1:T(8,128)(2,1)S(1)}, bf16[128,1,128]{2,0,1:T(8,128)(2,1)S(1)}, u32[]{:S(2)}, u32[]{:S(2)}) collective-permute-start(bf16[128,1,128]{2,0,1:T(8,128)(2,1)S(1)} %copy.67), channel_id=1, source_target_pairs={{0,32},{32,64},{64,96},{96,128},{128,160},{160,192},{192,224},{224... | collective-permute-start | bytes 98312 | tf_op jit(solution)/shard_map/while/body/eval_jaxpr/ppermute | solution.py:15
  66.7 15.1 %collective-permute-start.2 = (s32[1]{0:T(128)}, s32[1]{0:T(128)}, u32[]{:S(2)}, u32[]{:S(2)}) collective-permute-start(s32[1]{0:T(128)} %copy.68), channel_id=1, source_target_pairs={{0,32},{32,64},{64,96},{96,128},{128,160},{160,192},{192,224},{224... | collective-permute-start | bytes 20 | tf_op jit(solution)/shard_map/while/body/eval_jaxpr/ppermute | solution.py:15
  89.6 28.9 %collective-permute-start = (bf16[128,1,128]{2,0,1:T(8,128)(2,1)S(1)}, bf16[128,1,128]{2,0,1:T(8,128)(2,1)S(1)}, u32[]{:S(2)}, u32[]{:S(2)}) collective-permute-start(bf16[128,1,128]{2,0,1:T(8,128)(2,1)S(1)} %copy.66), channel_id=1, source_target_pairs={{0,32},{32,64},{64,96},{96,128},{128,160},{160,192},{192,224},{224... | collective-permute-start | bytes 98312 | tf_op jit(solution)/shard_map/while/body/eval_jaxpr/ppermute | solution.py:15
  94.6 23.9 %collective-permute-start.1 = (bf16[128,1,128]{2,0,1:T(8,128)(2,1)S(1)}, bf16[128,1,128]{2,0,1:T(8,128)(2,1)S(1)}, u32[]{:S(2)}, u32[]{:S(2)}) collective-permute-start(bf16[128,1,128]{2,0,1:T(8,128)(2,1)S(1)} %copy.67), channel_id=1, source_target_pairs={{0,32},{32,64},{64,96},{96,128},{128,160},{160,192},{192,224},{224... | collective-permute-start | bytes 98312 | tf_op jit(solution)/shard_map/while/body/eval_jaxpr/ppermute | solution.py:15
  103.5 15.0 %collective-permute-start.2 = (s32[1]{0:T(128)}, s32[1]{0:T(128)}, u32[]{:S(2)}, u32[]{:S(2)}) collective-permute-start(s32[1]{0:T(128)} %copy.68), channel_id=1, source_target_pairs={{0,32},{32,64},{64,96},{96,128},{128,160},{160,192},{192,224},{224... | collective-permute-start | bytes 20 | tf_op jit(solution)/shard_map/while/body/eval_jaxpr/ppermute | solution.py:15
  125.8 30.1 %collective-permute-start = (bf16[128,1,128]{2,0,1:T(8,128)(2,1)S(1)}, bf16[128,1,128]{2,0,1:T(8,128)(2,1)S(1)}, u32[]{:S(2)}, u32[]{:S(2)}) collective-permute-start(bf16[128,1,128]{2,0,1:T(8,128)(2,1)S(1)} %copy.66), channel_id=1, source_target_pairs={{0,32},{32,64},{64,96},{96,128},{128,160},{160,192},{192,224},{224... | collective-permute-start | bytes 98312 | tf_op jit(solution)/shard_map/while/body/eval_jaxpr/ppermute | solution.py:15
  134.1 21.8 %collective-permute-start.1 = (bf16[128,1,128]{2,0,1:T(8,128)(2,1)S(1)}, bf16[128,1,128]{2,0,1:T(8,128)(2,1)S(1)}, u32[]{:S(2)}, u32[]{:S(2)}) collective-permute-start(bf16[128,1,128]{2,0,1:T(8,128)(2,1)S(1)} %copy.67), channel_id=1, source_target_pairs={{0,32},{32,64},{64,96},{96,128},{128,160},{160,192},{192,224},{224... | collective-permute-start | bytes 98312 | tf_op jit(solution)/shard_map/while/body/eval_jaxpr/ppermute | solution.py:15
  138.2 17.6 %collective-permute-start.2 = (s32[1]{0:T(128)}, s32[1]{0:T(128)}, u32[]{:S(2)}, u32[]{:S(2)}) collective-permute-start(s32[1]{0:T(128)} %copy.68), channel_id=1, source_target_pairs={{0,32},{32,64},{64,96},{96,128},{128,160},{160,192},{192,224},{224... | collective-permute-start | bytes 20 | tf_op jit(solution)/shard_map/while/body/eval_jaxpr/ppermute | solution.py:15
  160.6 30.4 %collective-permute-start = (bf16[128,1,128]{2,0,1:T(8,128)(2,1)S(1)}, bf16[128,1,128]{2,0,1:T(8,128)(2,1)S(1)}, u32[]{:S(2)}, u32[]{:S(2)}) collective-permute-start(bf16[128,1,128]{2,0,1:T(8,128)(2,1)S(1)} %copy.66), channel_id=1, source_target_pairs={{0,32},{32,64},{64,96},{96,128},{128,160},{160,192},{192,224},{224... | collective-permute-start | bytes 98312 | tf_op jit(solution)/shard_map/while/body/eval_jaxpr/ppermute | solution.py:15
  166.6 24.4 %collective-permute-start.1 = (bf16[128,1,128]{2,0,1:T(8,128)(2,1)S(1)}, bf16[128,1,128]{2,0,1:T(8,128)(2,1)S(1)}, u32[]{:S(2)}, u32[]{:S(2)}) collective-permute-start(bf16[128,1,128]{2,0,1:T(8,128)(2,1)S(1)} %copy.67), channel_id=1, source_target_pairs={{0,32},{32,64},{64,96},{96,128},{128,160},{160,192},{192,224},{224... | collective-permute-start | bytes 98312 | tf_op jit(solution)/shard_map/while/body/eval_jaxpr/ppermute | solution.py:15
  173.7 17.4 %collective-permute-start.2 = (s32[1]{0:T(128)}, s32[1]{0:T(128)}, u32[]{:S(2)}, u32[]{:S(2)}) collective-permute-start(s32[1]{0:T(128)} %copy.68), channel_id=1, source_target_pairs={{0,32},{32,64},{64,96},{96,128},{128,160},{160,192},{192,224},{224... | collective-permute-start | bytes 20 | tf_op jit(solution)/shard_map/while/body/eval_jaxpr/ppermute | solution.py:15
  198.3 27.4 %collective-permute-start = (bf16[128,1,128]{2,0,1:T(8,128)(2,1)S(1)}, bf16[128,1,128]{2,0,1:T(8,128)(2,1)S(1)}, u32[]{:S(2)}, u32[]{:S(2)}) collective-permute-start(bf16[128,1,128]{2,0,1:T(8,128)(2,1)S(1)} %copy.66), channel_id=1, source_target_pairs={{0,32},{32,64},{64,96},{96,128},{128,160},{160,192},{192,224},{224... | collective-permute-start | bytes 98312 | tf_op jit(solution)/shard_map/while/body/eval_jaxpr/ppermute | solution.py:15
  201.6 24.1 %collective-permute-start.1 = (bf16[128,1,128]{2,0,1:T(8,128)(2,1)S(1)}, bf16[128,1,128]{2,0,1:T(8,128)(2,1)S(1)}, u32[]{:S(2)}, u32[]{:S(2)}) collective-permute-start(bf16[128,1,128]{2,0,1:T(8,128)(2,1)S(1)} %copy.67), channel_id=1, source_target_pairs={{0,32},{32,64},{64,96},{96,128},{128,160},{160,192},{192,224},{224... | collective-permute-start | bytes 98312 | tf_op jit(solution)/shard_map/while/body/eval_jaxpr/ppermute | solution.py:15
  208.6 17.0 %collective-permute-start.2 = (s32[1]{0:T(128)}, s32[1]{0:T(128)}, u32[]{:S(2)}, u32[]{:S(2)}) collective-permute-start(s32[1]{0:T(128)} %copy.68), channel_id=1, source_target_pairs={{0,32},{32,64},{64,96},{96,128},{128,160},{160,192},{192,224},{224... | collective-permute-start | bytes 20 | tf_op jit(solution)/shard_map/while/body/eval_jaxpr/ppermute | solution.py:15
  233.6 29.4 %collective-permute-start = (bf16[128,1,128]{2,0,1:T(8,128)(2,1)S(1)}, bf16[128,1,128]{2,0,1:T(8,128)(2,1)S(1)}, u32[]{:S(2)}, u32[]{:S(2)}) collective-permute-start(bf16[128,1,128]{2,0,1:T(8,128)(2,1)S(1)} %copy.66), channel_id=1, source_target_pairs={{0,32},{32,64},{64,96},{96,128},{128,160},{160,192},{192,224},{224... | collective-permute-start | bytes 98312 | tf_op jit(solution)/shard_map/while/body/eval_jaxpr/ppermute | solution.py:15
  236.2 26.9 %collective-permute-start.1 = (bf16[128,1,128]{2,0,1:T(8,128)(2,1)S(1)}, bf16[128,1,128]{2,0,1:T(8,128)(2,1)S(1)}, u32[]{:S(2)}, u32[]{:S(2)}) collective-permute-start(bf16[128,1,128]{2,0,1:T(8,128)(2,1)S(1)} %copy.67), channel_id=1, source_target_pairs={{0,32},{32,64},{64,96},{96,128},{128,160},{160,192},{192,224},{224... | collective-permute-start | bytes 98312 | tf_op jit(solution)/shard_map/while/body/eval_jaxpr/ppermute | solution.py:15
  242.8 20.2 %collective-permute-start.2 = (s32[1]{0:T(128)}, s32[1]{0:T(128)}, u32[]{:S(2)}, u32[]{:S(2)}) collective-permute-start(s32[1]{0:T(128)} %copy.68), channel_id=1, source_target_pairs={{0,32},{32,64},{64,96},{96,128},{128,160},{160,192},{192,224},{224... | collective-permute-start | bytes 20 | tf_op jit(solution)/shard_map/while/body/eval_jaxpr/ppermute | solution.py:15
  247.4 15.6 %collective-permute-start.3 = (f32[128,1,128]{2,0,1:T(8,128)S(1)}, f32[128,1,128]{2,0,1:T(8,128)S(1)}, u32[]{:S(2)}, u32[]{:S(2)}) collective-permute-start(f32[128,1,128]{2,0,1:T(8,128)S(1)} %fusion.89), channel_id=1, source_target_pairs={{0,32},{32,64},{64,96},{96,128},{128,160},{160,192},{192,224},{224... | collective-permute-start | bytes 196616 | tf_op jit(solution)/shard_map/while/body/eval_jaxpr/ppermute | solution.py:15
  266.0 31.5 %collective-permute-start = (bf16[128,1,128]{2,0,1:T(8,128)(2,1)S(1)}, bf16[128,1,128]{2,0,1:T(8,128)(2,1)S(1)}, u32[]{:S(2)}, u32[]{:S(2)}) collective-permute-start(bf16[128,1,128]{2,0,1:T(8,128)(2,1)S(1)} %copy.66), channel_id=1, source_target_pairs={{0,32},{32,64},{64,96},{96,128},{128,160},{160,192},{192,224},{224... | collective-permute-start | bytes 98312 | tf_op jit(solution)/shard_map/while/body/eval_jaxpr/ppermute | solution.py:15
  272.8 24.7 %collective-permute-start.1 = (bf16[128,1,128]{2,0,1:T(8,128)(2,1)S(1)}, bf16[128,1,128]{2,0,1:T(8,128)(2,1)S(1)}, u32[]{:S(2)}, u32[]{:S(2)}) collective-permute-start(bf16[128,1,128]{2,0,1:T(8,128)(2,1)S(1)} %copy.67), channel_id=1, source_target_pairs={{0,32},{32,64},{64,96},{96,128},{128,160},{160,192},{192,224},{224... | collective-permute-start | bytes 98312 | tf_op jit(solution)/shard_map/while/body/eval_jaxpr/ppermute | solution.py:15
  279.3 18.2 %collective-permute-start.2 = (s32[1]{0:T(128)}, s32[1]{0:T(128)}, u32[]{:S(2)}, u32[]{:S(2)}) collective-permute-start(s32[1]{0:T(128)} %copy.68), channel_id=1, source_target_pairs={{0,32},{32,64},{64,96},{96,128},{128,160},{160,192},{192,224},{224... | collective-permute-start | bytes 20 | tf_op jit(solution)/shard_map/while/body/eval_jaxpr/ppermute | solution.py:15
  305.3 25.5 %collective-permute-start = (bf16[128,1,128]{2,0,1:T(8,128)(2,1)S(1)}, bf16[128,1,128]{2,0,1:T(8,128)(2,1)S(1)}, u32[]{:S(2)}, u32[]{:S(2)}) collective-permute-start(bf16[128,1,128]{2,0,1:T(8,128)(2,1)S(1)} %copy.66), channel_id=1, source_target_pairs={{0,32},{32,64},{64,96},{96,128},{128,160},{160,192},{192,224},{224... | collective-permute-start | bytes 98312 | tf_op jit(solution)/shard_map/while/body/eval_jaxpr/ppermute | solution.py:15
  308.2 22.6 %collective-permute-start.1 = (bf16[128,1,128]{2,0,1:T(8,128)(2,1)S(1)}, bf16[128,1,128]{2,0,1:T(8,128)(2,1)S(1)}, u32[]{:S(2)}, u32[]{:S(2)}) collective-permute-start(bf16[128,1,128]{2,0,1:T(8,128)(2,1)S(1)} %copy.67), channel_id=1, source_target_pairs={{0,32},{32,64},{64,96},{96,128},{128,160},{160,192},{192,224},{224... | collective-permute-start | bytes 98312 | tf_op jit(solution)/shard_map/while/body/eval_jaxpr/ppermute | solution.py:15
  340.0 27.1 %collective-permute-start = (bf16[128,1,128]{2,0,1:T(8,128)(2,1)S(1)}, bf16[128,1,128]{2,0,1:T(8,128)(2,1)S(1)}, u32[]{:S(2)}, u32[]{:S(2)}) collective-permute-start(bf16[128,1,128]{2,0,1:T(8,128)(2,1)S(1)} %copy.66), channel_id=1, source_target_pairs={{0,32},{32,64},{64,96},{96,128},{128,160},{160,192},{192,224},{224... | collective-permute-start | bytes 98312 | tf_op jit(solution)/shard_map/while/body/eval_jaxpr/ppermute | solution.py:15
  341.9 25.1 %collective-permute-start.1 = (bf16[128,1,128]{2,0,1:T(8,128)(2,1)S(1)}, bf16[128,1,128]{2,0,1:T(8,128)(2,1)S(1)}, u32[]{:S(2)}, u32[]{:S(2)}) collective-permute-start(bf16[128,1,128]{2,0,1:T(8,128)(2,1)S(1)} %copy.67), channel_id=1, source_target_pairs={{0,32},{32,64},{64,96},{96,128},{128,160},{160,192},{192,224},{224... | collective-permute-start | bytes 98312 | tf_op jit(solution)/shard_map/while/body/eval_jaxpr/ppermute | solution.py:15
  349.8 17.2 %collective-permute-start.2 = (s32[1]{0:T(128)}, s32[1]{0:T(128)}, u32[]{:S(2)}, u32[]{:S(2)}) collective-permute-start(s32[1]{0:T(128)} %copy.68), channel_id=1, source_target_pairs={{0,32},{32,64},{64,96},{96,128},{128,160},{160,192},{192,224},{224... | collective-permute-start | bytes 20 | tf_op jit(solution)/shard_map/while/body/eval_jaxpr/ppermute | solution.py:15
  375.7 29.3 %collective-permute-start = (bf16[128,1,128]{2,0,1:T(8,128)(2,1)S(1)}, bf16[128,1,128]{2,0,1:T(8,128)(2,1)S(1)}, u32[]{:S(2)}, u32[]{:S(2)}) collective-permute-start(bf16[128,1,128]{2,0,1:T(8,128)(2,1)S(1)} %copy.66), channel_id=1, source_target_pairs={{0,32},{32,64},{64,96},{96,128},{128,160},{160,192},{192,224},{224... | collective-permute-start | bytes 98312 | tf_op jit(solution)/shard_map/while/body/eval_jaxpr/ppermute | solution.py:15
  378.6 26.4 %collective-permute-start.1 = (bf16[128,1,128]{2,0,1:T(8,128)(2,1)S(1)}, bf16[128,1,128]{2,0,1:T(8,128)(2,1)S(1)}, u32[]{:S(2)}, u32[]{:S(2)}) collective-permute-start(bf16[128,1,128]{2,0,1:T(8,128)(2,1)S(1)} %copy.67), channel_id=1, source_target_pairs={{0,32},{32,64},{64,96},{96,128},{128,160},{160,192},{192,224},{224... | collective-permute-start | bytes 98312 | tf_op jit(solution)/shard_map/while/body/eval_jaxpr/ppermute | solution.py:15
  384.5 20.5 %collective-permute-start.2 = (s32[1]{0:T(128)}, s32[1]{0:T(128)}, u32[]{:S(2)}, u32[]{:S(2)}) collective-permute-start(s32[1]{0:T(128)} %copy.68), channel_id=1, source_target_pairs={{0,32},{32,64},{64,96},{96,128},{128,160},{160,192},{192,224},{224... | collective-permute-start | bytes 20 | tf_op jit(solution)/shard_map/while/body/eval_jaxpr/ppermute | solution.py:15
  410.8 30.8 %collective-permute-start = (bf16[128,1,128]{2,0,1:T(8,128)(2,1)S(1)}, bf16[128,1,128]{2,0,1:T(8,128)(2,1)S(1)}, u32[]{:S(2)}, u32[]{:S(2)}) collective-permute-start(bf16[128,1,128]{2,0,1:T(8,128)(2,1)S(1)} %copy.66), channel_id=1, source_target_pairs={{0,32},{32,64},{64,96},{96,128},{128,160},{160,192},{192,224},{224... | collective-permute-start | bytes 98312 | tf_op jit(solution)/shard_map/while/body/eval_jaxpr/ppermute | solution.py:15
  415.0 26.7 %collective-permute-start.1 = (bf16[128,1,128]{2,0,1:T(8,128)(2,1)S(1)}, bf16[128,1,128]{2,0,1:T(8,128)(2,1)S(1)}, u32[]{:S(2)}, u32[]{:S(2)}) collective-permute-start(bf16[128,1,128]{2,0,1:T(8,128)(2,1)S(1)} %copy.67), channel_id=1, source_target_pairs={{0,32},{32,64},{64,96},{96,128},{128,160},{160,192},{192,224},{224... | collective-permute-start | bytes 98312 | tf_op jit(solution)/shard_map/while/body/eval_jaxpr/ppermute | solution.py:15
  422.8 18.8 %collective-permute-start.2 = (s32[1]{0:T(128)}, s32[1]{0:T(128)}, u32[]{:S(2)}, u32[]{:S(2)}) collective-permute-start(s32[1]{0:T(128)} %copy.68), channel_id=1, source_target_pairs={{0,32},{32,64},{64,96},{96,128},{128,160},{160,192},{192,224},{224... | collective-permute-start | bytes 20 | tf_op jit(solution)/shard_map/while/body/eval_jaxpr/ppermute | solution.py:15
  446.3 26.8 %collective-permute-start = (bf16[128,1,128]{2,0,1:T(8,128)(2,1)S(1)}, bf16[128,1,128]{2,0,1:T(8,128)(2,1)S(1)}, u32[]{:S(2)}, u32[]{:S(2)}) collective-permute-start(bf16[128,1,128]{2,0,1:T(8,128)(2,1)S(1)} %copy.66), channel_id=1, source_target_pairs={{0,32},{32,64},{64,96},{96,128},{128,160},{160,192},{192,224},{224... | collective-permute-start | bytes 98312 | tf_op jit(solution)/shard_map/while/body/eval_jaxpr/ppermute | solution.py:15
  452.8 20.3 %collective-permute-start.1 = (bf16[128,1,128]{2,0,1:T(8,128)(2,1)S(1)}, bf16[128,1,128]{2,0,1:T(8,128)(2,1)S(1)}, u32[]{:S(2)}, u32[]{:S(2)}) collective-permute-start(bf16[128,1,128]{2,0,1:T(8,128)(2,1)S(1)} %copy.67), channel_id=1, source_target_pairs={{0,32},{32,64},{64,96},{96,128},{128,160},{160,192},{192,224},{224... | collective-permute-start | bytes 98312 | tf_op jit(solution)/shard_map/while/body/eval_jaxpr/ppermute | solution.py:15
  482.7 25.7 %collective-permute-start = (bf16[128,1,128]{2,0,1:T(8,128)(2,1)S(1)}, bf16[128,1,128]{2,0,1:T(8,128)(2,1)S(1)}, u32[]{:S(2)}, u32[]{:S(2)}) collective-permute-start(bf16[128,1,128]{2,0,1:T(8,128)(2,1)S(1)} %copy.66), channel_id=1, source_target_pairs={{0,32},{32,64},{64,96},{96,128},{128,160},{160,192},{192,224},{224... | collective-permute-start | bytes 98312 | tf_op jit(solution)/shard_map/while/body/eval_jaxpr/ppermute | solution.py:15
  484.6 23.8 %collective-permute-start.1 = (bf16[128,1,128]{2,0,1:T(8,128)(2,1)S(1)}, bf16[128,1,128]{2,0,1:T(8,128)(2,1)S(1)}, u32[]{:S(2)}, u32[]{:S(2)}) collective-permute-start(bf16[128,1,128]{2,0,1:T(8,128)(2,1)S(1)} %copy.67), channel_id=1, source_target_pairs={{0,32},{32,64},{64,96},{96,128},{128,160},{160,192},{192,224},{224... | collective-permute-start | bytes 98312 | tf_op jit(solution)/shard_map/while/body/eval_jaxpr/ppermute | solution.py:15
  490.0 18.4 %collective-permute-start.2 = (s32[1]{0:T(128)}, s32[1]{0:T(128)}, u32[]{:S(2)}, u32[]{:S(2)}) collective-permute-start(s32[1]{0:T(128)} %copy.68), channel_id=1, source_target_pairs={{0,32},{32,64},{64,96},{96,128},{128,160},{160,192},{192,224},{224... | collective-permute-start | bytes 20 | tf_op jit(solution)/shard_map/while/body/eval_jaxpr/ppermute | solution.py:15
  518.8 25.9 %collective-permute-start = (bf16[128,1,128]{2,0,1:T(8,128)(2,1)S(1)}, bf16[128,1,128]{2,0,1:T(8,128)(2,1)S(1)}, u32[]{:S(2)}, u32[]{:S(2)}) collective-permute-start(bf16[128,1,128]{2,0,1:T(8,128)(2,1)S(1)} %copy.66), channel_id=1, source_target_pairs={{0,32},{32,64},{64,96},{96,128},{128,160},{160,192},{192,224},{224... | collective-permute-start | bytes 98312 | tf_op jit(solution)/shard_map/while/body/eval_jaxpr/ppermute | solution.py:15
  520.7 24.0 %collective-permute-start.1 = (bf16[128,1,128]{2,0,1:T(8,128)(2,1)S(1)}, bf16[128,1,128]{2,0,1:T(8,128)(2,1)S(1)}, u32[]{:S(2)}, u32[]{:S(2)}) collective-permute-start(bf16[128,1,128]{2,0,1:T(8,128)(2,1)S(1)} %copy.67), channel_id=1, source_target_pairs={{0,32},{32,64},{64,96},{96,128},{128,160},{160,192},{192,224},{224... | collective-permute-start | bytes 98312 | tf_op jit(solution)/shard_map/while/body/eval_jaxpr/ppermute | solution.py:15
  523.2 21.5 %collective-permute-start.2 = (s32[1]{0:T(128)}, s32[1]{0:T(128)}, u32[]{:S(2)}, u32[]{:S(2)}) collective-permute-start(s32[1]{0:T(128)} %copy.68), channel_id=1, source_target_pairs={{0,32},{32,64},{64,96},{96,128},{128,160},{160,192},{192,224},{224... | collective-permute-start | bytes 20 | tf_op jit(solution)/shard_map/while/body/eval_jaxpr/ppermute | solution.py:15
  567.0 268.3 %all-reduce.2.cloned.1.call-start = ((), (), s32[]{:S(2)}) async-start(), calls=%async_computation | async-start | bytes 327680 | tf_op jit(solution)/shard_map/psum | solution.py:148
  567.3 70.6 %collective-permute-start.6 = (bf16[128,1,128]{2,0,1:T(8,128)(2,1)S(1)}, bf16[128,1,128]{2,0,1:T(8,128)(2,1)S(1)}, u32[]{:S(2)}, u32[]{:S(2)}) collective-permute-start(bf16[128,1,128]{2,0,1:T(8,128)(2,1)S(1)} %fusion.33), channel_id=1, source_target_pairs={{0,32},{32,64},{64,96},{96,128},{128,160},{160,192},{192,224},{224... | collective-permute-start | bytes 98312 | tf_op jit(solution)/shard_map/ppermute | solution.py:15
  (41 other events, 1141.5 us)
Sparse Core Ops, SparseCore 0:
  567.1 66.7 all-gather.2
  637.4 197.8 all-reduce.1
where the time goes:
time: 848 us; the launch traced here: 845 us
  starting transfers between devices  396 us (47%)
  waiting for transfers between devices  381 us (45%)
  matrix products  19.6 us (2%)
  between operations  14.8 us (2%)
  other arithmetic  12.4 us (1%)
  local copies, waits for them, and re-layouts  10.7 us (1%)
  loops' own time  10.2 us (1%)
    ppermute x77, starting transfers between devices, from_behind(): return lax.ppermute(value, axis, pairs)  396 us
    psum x1, waiting for transfers between devices, local(): grad_wk = lax.psum(summed, 'ctx')  197 us
    ppermute x77, waiting for transfers between devices, from_behind(): return lax.ppermute(value, axis, pairs)  120 us
    all_gather x1, waiting for transfers between devices, local(): piece = lax.all_gather(key_gradient[None], 'fsdp', axis=0, tiled=True)  63.8 us
  transfers between devices with their start and end apart: 79, of which 30 were waited for; matrix products, arithmetic and copies ran while one was open for 4% of the time, Pallas kernels for 0%

commit v1 on v0

--- a/solution.py
+++ b/solution.py
@@ -7,6 +7,12 @@
 KEY_VALUE_HEADS = 4
 HEAD_SIZE = 128
 HEAD_GROUPS = 4
+
+
+def gather_and_add(x, mesh_axis):
+    parts = lax.all_gather(x, mesh_axis, axis=0, tiled=False)
+    total = parts.sum(axis=0)
+    return total
 
 
 def from_behind(value, axis, steps):
@@ -145,7 +151,7 @@
     placing = (group_ids[:, None] == lax.iota(jnp.int32, HEAD_GROUPS)[None, :]).astype(jnp.float32)
     summed = jnp.einsum("pij,pr->irj", rounded, placing)
     summed = summed.reshape(feature_cols, HEAD_GROUPS * local_width)
-    grad_wk = lax.psum(summed, "ctx")
+    grad_wk = gather_and_add(summed, "ctx")
     return (grad_q[None], key_gradient[None], value_gradient[None], grad_wk)
 
 

time: 848 us -> 756 us (0.89)
  the two profiles are of different devices: /device:TPU:2 before, /device:TPU:1 now
where the time goes in v1:
time: 756 us; the launch traced here: 753 us
  waiting for transfers between devices  347 us (46%)
  starting transfers between devices  336 us (44%)
  matrix products  19.6 us (3%)
  other arithmetic  15.7 us (2%)
  between operations  14.8 us (2%)
  loops' own time  10.3 us (1%)
  local copies, waits for them, and re-layouts  10.2 us (1%)
    ppermute x77, starting transfers between devices, from_behind(): return lax.ppermute(value, axis, pairs)  335 us
    ppermute x77, waiting for transfers between devices, from_behind(): return lax.ppermute(value, axis, pairs)  148 us
    all_gather x1, waiting for transfers between devices, local(): piece = lax.all_gather(key_gradient[None], 'fsdp', axis=0, tiled=True)  106 us
    all_gather x1, waiting for transfers between devices, gather_and_add(): parts = lax.all_gather(x, mesh_axis, axis=0, tiled=False)  93.4 us
  transfers between devices with their start and end apart: 79, of which 30 were waited for; matrix products, arithmetic and copies ran while one was open for 4% of the time, Pallas kernels for 0%

profile of v1, /device:TPU:1, one launch (start us, length us, event | category | flops | bytes accessed | tf_op | source)
XLA Modules:
  0.0 753.3 jit_solution(16213953933261884513)
XLA Ops:
  14.4 500.8 %while.23 = (s32[]{:T(128)}, f32[128,1,5,128]{3,0,2,1:T(8,128)S(1)}, bf16[128,1,128]{2,0,1:T(8,128)(2,1)S(1)}, bf16[128,1,128]{2,0,1:T(8,128)(2,1)S(1)}, s32[1]{...) while((s32[]{:T(128)}, ...), condition=%wide.region_2.3_spmd.clone, body=%wide.region_1.2_spmd.clone.sunk | while | flops 105726208 | bytes 4103563 | solution.py:133
  14.4 9.6 %collective-permute-start = (bf16[128,1,128]{2,0,1:T(8,128)(2,1)S(1)}, bf16[128,1,128]{2,0,1:T(8,128)(2,1)S(1)}, u32[]{:S(2)}, u32[]{:S(2)}) collective-permute-start(bf16[128,1,128]{2,0,1:T(8,128)(2,1)S(1)} %copy.80), channel_id=1, source_target_pairs={{0,32},{32,64},{64,96},{96,128},{128,160},{160,192},{192,224},{224... | collective-permute-start | bytes 98312 | tf_op jit(solution)/shard_map/while/body/eval_jaxpr/ppermute | solution.py:21
  24.1 8.8 %collective-permute-start.1 = (bf16[128,1,128]{2,0,1:T(8,128)(2,1)S(1)}, bf16[128,1,128]{2,0,1:T(8,128)(2,1)S(1)}, u32[]{:S(2)}, u32[]{:S(2)}) collective-permute-start(bf16[128,1,128]{2,0,1:T(8,128)(2,1)S(1)} %copy.81), channel_id=1, source_target_pairs={{0,32},{32,64},{64,96},{96,128},{128,160},{160,192},{192,224},{224... | collective-permute-start | bytes 98312 | tf_op jit(solution)/shard_map/while/body/eval_jaxpr/ppermute | solution.py:21
  33.5 4.7 collective-permute-start.2
  41.7 4.6 collective-permute-start.4
  46.6 4.3 collective-permute-done.3
  57.0 8.9 %collective-permute-start.1 = (bf16[128,1,128]{2,0,1:T(8,128)(2,1)S(1)}, bf16[128,1,128]{2,0,1:T(8,128)(2,1)S(1)}, u32[]{:S(2)}, u32[]{:S(2)}) collective-permute-start(bf16[128,1,128]{2,0,1:T(8,128)(2,1)S(1)} %copy.81), channel_id=1, source_target_pairs={{0,32},{32,64},{64,96},{96,128},{128,160},{160,192},{192,224},{224... | collective-permute-start | bytes 98312 | tf_op jit(solution)/shard_map/while/body/eval_jaxpr/ppermute | solution.py:21
  71.3 4.4 collective-permute-start.3
  82.3 6.1 collective-permute-done.4
  90.3 7.0 collective-permute-start.1
  102.4 5.7 collective-permute-start.3
  114.1 6.8 collective-permute-done.4
  122.8 6.2 collective-permute-start.1
  133.6 7.9 %collective-permute-start.3 = (f32[128,1,128]{2,0,1:T(8,128)S(1)}, f32[128,1,128]{2,0,1:T(8,128)S(1)}, u32[]{:S(2)}, u32[]{:S(2)}) collective-permute-start(f32[128,1,128]{2,0,1:T(8,128)S(1)} %fusion.87), channel_id=1, source_target_pairs={{0,32},{32,64},{64,96},{96,128},{128,160},{160,192},{192,224},{224... | collective-permute-start | bytes 196616 | tf_op jit(solution)/shard_map/while/body/eval_jaxpr/ppermute | solution.py:21
  145.1 9.7 %collective-permute-done.4 = f32[128,1,128]{2,0,1:T(8,128)S(1)} collective-permute-done((f32[128,1,128]{2,0,1:T(8,128)S(1)}, f32[128,1,128]{2,0,1:T(8,128)S(1)}, u32[]{:S(2)}, u32[]{:S(2)}) %collective-permute-start.4) | collective-permute-done | bytes 65568 | tf_op jit(solution)/shard_map/while/body/eval_jaxpr/ppermute | solution.py:21
  164.7 9.5 %collective-permute-start.3 = (f32[128,1,128]{2,0,1:T(8,128)S(1)}, f32[128,1,128]{2,0,1:T(8,128)S(1)}, u32[]{:S(2)}, u32[]{:S(2)}) collective-permute-start(f32[128,1,128]{2,0,1:T(8,128)S(1)} %fusion.87), channel_id=1, source_target_pairs={{0,32},{32,64},{64,96},{96,128},{128,160},{160,192},{192,224},{224... | collective-permute-start | bytes 196616 | tf_op jit(solution)/shard_map/while/body/eval_jaxpr/ppermute | solution.py:21
  177.7 8.8 %collective-permute-done.4 = f32[128,1,128]{2,0,1:T(8,128)S(1)} collective-permute-done((f32[128,1,128]{2,0,1:T(8,128)S(1)}, f32[128,1,128]{2,0,1:T(8,128)S(1)}, u32[]{:S(2)}, u32[]{:S(2)}) %collective-permute-start.4) | collective-permute-done | bytes 65568 | tf_op jit(solution)/shard_map/while/body/eval_jaxpr/ppermute | solution.py:21
  188.5 5.7 collective-permute-start.1
  200.0 8.0 %collective-permute-start.3 = (f32[128,1,128]{2,0,1:T(8,128)S(1)}, f32[128,1,128]{2,0,1:T(8,128)S(1)}, u32[]{:S(2)}, u32[]{:S(2)}) collective-permute-start(f32[128,1,128]{2,0,1:T(8,128)S(1)} %fusion.87), channel_id=1, source_target_pairs={{0,32},{32,64},{64,96},{96,128},{128,160},{160,192},{192,224},{224... | collective-permute-start | bytes 196616 | tf_op jit(solution)/shard_map/while/body/eval_jaxpr/ppermute | solution.py:21
  211.4 11.2 %collective-permute-done.4 = f32[128,1,128]{2,0,1:T(8,128)S(1)} collective-permute-done((f32[128,1,128]{2,0,1:T(8,128)S(1)}, f32[128,1,128]{2,0,1:T(8,128)S(1)}, u32[]{:S(2)}, u32[]{:S(2)}) %collective-permute-start.4) | collective-permute-done | bytes 65568 | tf_op jit(solution)/shard_map/while/body/eval_jaxpr/ppermute | solution.py:21
  231.4 10.2 %collective-permute-start.3 = (f32[128,1,128]{2,0,1:T(8,128)S(1)}, f32[128,1,128]{2,0,1:T(8,128)S(1)}, u32[]{:S(2)}, u32[]{:S(2)}) collective-permute-start(f32[128,1,128]{2,0,1:T(8,128)S(1)} %fusion.87), channel_id=1, source_target_pairs={{0,32},{32,64},{64,96},{96,128},{128,160},{160,192},{192,224},{224... | collective-permute-start | bytes 196616 | tf_op jit(solution)/shard_map/while/body/eval_jaxpr/ppermute | solution.py:21
  244.0 8.8 %collective-permute-done.4 = f32[128,1,128]{2,0,1:T(8,128)S(1)} collective-permute-done((f32[128,1,128]{2,0,1:T(8,128)S(1)}, f32[128,1,128]{2,0,1:T(8,128)S(1)}, u32[]{:S(2)}, u32[]{:S(2)}) %collective-permute-start.4) | collective-permute-done | bytes 65568 | tf_op jit(solution)/shard_map/while/body/eval_jaxpr/ppermute | solution.py:21
  257.2 10.7 %collective-permute-start.2 = (s32[1]{0:T(128)}, s32[1]{0:T(128)}, u32[]{:S(2)}, u32[]{:S(2)}) collective-permute-start(s32[1]{0:T(128)} %copy.82), channel_id=1, source_target_pairs={{0,32},{32,64},{64,96},{96,128},{128,160},{160,192},{192,224},{224... | collective-permute-start | bytes 20 | tf_op jit(solution)/shard_map/while/body/eval_jaxpr/ppermute | solution.py:21
  269.3 9.1 %collective-permute-start.3 = (f32[128,1,128]{2,0,1:T(8,128)S(1)}, f32[128,1,128]{2,0,1:T(8,128)S(1)}, u32[]{:S(2)}, u32[]{:S(2)}) collective-permute-start(f32[128,1,128]{2,0,1:T(8,128)S(1)} %fusion.87), channel_id=1, source_target_pairs={{0,32},{32,64},{64,96},{96,128},{128,160},{160,192},{192,224},{224... | collective-permute-start | bytes 196616 | tf_op jit(solution)/shard_map/while/body/eval_jaxpr/ppermute | solution.py:21
  281.6 12.4 %collective-permute-done.4 = f32[128,1,128]{2,0,1:T(8,128)S(1)} collective-permute-done((f32[128,1,128]{2,0,1:T(8,128)S(1)}, f32[128,1,128]{2,0,1:T(8,128)S(1)}, u32[]{:S(2)}, u32[]{:S(2)}) %collective-permute-start.4) | collective-permute-done | bytes 65568 | tf_op jit(solution)/shard_map/while/body/eval_jaxpr/ppermute | solution.py:21
  302.5 4.2 collective-permute-start.3
  309.2 4.4 collective-permute-done.3
  313.5 4.7 collective-permute-done.4
  323.0 11.5 %collective-permute-start.2 = (s32[1]{0:T(128)}, s32[1]{0:T(128)}, u32[]{:S(2)}, u32[]{:S(2)}) collective-permute-start(s32[1]{0:T(128)} %copy.82), channel_id=1, source_target_pairs={{0,32},{32,64},{64,96},{96,128},{128,160},{160,192},{192,224},{224... | collective-permute-start | bytes 20 | tf_op jit(solution)/shard_map/while/body/eval_jaxpr/ppermute | solution.py:21
  335.8 8.6 %collective-permute-start.3 = (f32[128,1,128]{2,0,1:T(8,128)S(1)}, f32[128,1,128]{2,0,1:T(8,128)S(1)}, u32[]{:S(2)}, u32[]{:S(2)}) collective-permute-start(f32[128,1,128]{2,0,1:T(8,128)S(1)} %fusion.87), channel_id=1, source_target_pairs={{0,32},{32,64},{64,96},{96,128},{128,160},{160,192},{192,224},{224... | collective-permute-start | bytes 196616 | tf_op jit(solution)/shard_map/while/body/eval_jaxpr/ppermute | solution.py:21
  348.6 7.9 %collective-permute-done.4 = f32[128,1,128]{2,0,1:T(8,128)S(1)} collective-permute-done((f32[128,1,128]{2,0,1:T(8,128)S(1)}, f32[128,1,128]{2,0,1:T(8,128)S(1)}, u32[]{:S(2)}, u32[]{:S(2)}) %collective-permute-start.4) | collective-permute-done | bytes 65568 | tf_op jit(solution)/shard_map/while/body/eval_jaxpr/ppermute | solution.py:21
  364.9 5.9 collective-permute-start.3
  376.0 6.6 collective-permute-done.4
  384.5 10.3 %collective-permute-start.1 = (bf16[128,1,128]{2,0,1:T(8,128)(2,1)S(1)}, bf16[128,1,128]{2,0,1:T(8,128)(2,1)S(1)}, u32[]{:S(2)}, u32[]{:S(2)}) collective-permute-start(bf16[128,1,128]{2,0,1:T(8,128)(2,1)S(1)} %copy.81), channel_id=1, source_target_pairs={{0,32},{32,64},{64,96},{96,128},{128,160},{160,192},{192,224},{224... | collective-permute-start | bytes 98312 | tf_op jit(solution)/shard_map/while/body/eval_jaxpr/ppermute | solution.py:21
  395.4 10.3 %collective-permute-start.2 = (s32[1]{0:T(128)}, s32[1]{0:T(128)}, u32[]{:S(2)}, u32[]{:S(2)}) collective-permute-start(s32[1]{0:T(128)} %copy.82), channel_id=1, source_target_pairs={{0,32},{32,64},{64,96},{96,128},{128,160},{160,192},{192,224},{224... | collective-permute-start | bytes 20 | tf_op jit(solution)/shard_map/while/body/eval_jaxpr/ppermute | solution.py:21
  407.1 9.1 %collective-permute-start.3 = (f32[128,1,128]{2,0,1:T(8,128)S(1)}, f32[128,1,128]{2,0,1:T(8,128)S(1)}, u32[]{:S(2)}, u32[]{:S(2)}) collective-permute-start(f32[128,1,128]{2,0,1:T(8,128)S(1)} %fusion.87), channel_id=1, source_target_pairs={{0,32},{32,64},{64,96},{96,128},{128,160},{160,192},{192,224},{224... | collective-permute-start | bytes 196616 | tf_op jit(solution)/shard_map/while/body/eval_jaxpr/ppermute | solution.py:21
  418.6 10.7 %collective-permute-done.4 = f32[128,1,128]{2,0,1:T(8,128)S(1)} collective-permute-done((f32[128,1,128]{2,0,1:T(8,128)S(1)}, f32[128,1,128]{2,0,1:T(8,128)S(1)}, u32[]{:S(2)}, u32[]{:S(2)}) %collective-permute-start.4) | collective-permute-done | bytes 65568 | tf_op jit(solution)/shard_map/while/body/eval_jaxpr/ppermute | solution.py:21
  444.4 5.1 collective-permute-done.3
  457.2 8.6 %collective-permute-start.2 = (s32[1]{0:T(128)}, s32[1]{0:T(128)}, u32[]{:S(2)}, u32[]{:S(2)}) collective-permute-start(s32[1]{0:T(128)} %copy.82), channel_id=1, source_target_pairs={{0,32},{32,64},{64,96},{96,128},{128,160},{160,192},{192,224},{224... | collective-permute-start | bytes 20 | tf_op jit(solution)/shard_map/while/body/eval_jaxpr/ppermute | solution.py:21
  467.3 7.4 collective-permute-start.3
  478.9 8.0 %collective-permute-done.4 = f32[128,1,128]{2,0,1:T(8,128)S(1)} collective-permute-done((f32[128,1,128]{2,0,1:T(8,128)S(1)}, f32[128,1,128]{2,0,1:T(8,128)S(1)}, u32[]{:S(2)}, u32[]{:S(2)}) %collective-permute-start.4) | collective-permute-done | bytes 65568 | tf_op jit(solution)/shard_map/while/body/eval_jaxpr/ppermute | solution.py:21
  495.3 8.4 %collective-permute-start.3 = (f32[128,1,128]{2,0,1:T(8,128)S(1)}, f32[128,1,128]{2,0,1:T(8,128)S(1)}, u32[]{:S(2)}, u32[]{:S(2)}) collective-permute-start(f32[128,1,128]{2,0,1:T(8,128)S(1)} %fusion.87), channel_id=1, source_target_pairs={{0,32},{32,64},{64,96},{96,128},{128,160},{160,192},{192,224},{224... | collective-permute-start | bytes 196616 | tf_op jit(solution)/shard_map/while/body/eval_jaxpr/ppermute | solution.py:21
  504.0 5.3 collective-permute-start.4
  509.7 5.5 collective-permute-done.4
  517.2 7.1 collective-permute-start.5
  529.4 106.0 %all-gather.6.cloned.1.call-done = bf16[4096,1,128]{2,0,1:T(8,128)(2,1)} async-done(((bf16[128,1,128]{2,0,1:T(8,128)(2,1)}), bf16[4096,1,128]{2,0,1:T(8,128)(2,1)}) %all-gather.6.cloned.1.call-update) | async-done | bytes 1048592 | tf_op jit(solution)/shard_map/all_gather | solution.py:143
  638.3 7.4 collective-permute-start.6
  649.2 93.4 %all-gather.4.cloned.1.call-done = f32[16,80,512]{2,1,0:T(8,128)} async-done(((f32[1,80,512]{2,1,0:T(8,128)}), f32[16,80,512]{2,1,0:T(8,128)}) %all-gather.4.cloned.1.call-update) | async-done | bytes 2621456 | tf_op jit(solution)/shard_map/all_gather | solution.py:13
  (302 shorter events, 182.9 us)
Async XLA Ops:
  7.2 628.2 %all-gather.6.cloned.1.call-start = ((), (), s32[]{:S(2)}) async-start(), calls=%async_computation.1 | async-start | bytes 1081344 | tf_op jit(solution)/shard_map/all_gather | solution.py:143
  14.4 32.2 %collective-permute-start = (bf16[128,1,128]{2,0,1:T(8,128)(2,1)S(1)}, bf16[128,1,128]{2,0,1:T(8,128)(2,1)S(1)}, u32[]{:S(2)}, u32[]{:S(2)}) collective-permute-start(bf16[128,1,128]{2,0,1:T(8,128)(2,1)S(1)} %copy.80), channel_id=1, source_target_pairs={{0,32},{32,64},{64,96},{96,128},{128,160},{160,192},{192,224},{224... | collective-permute-start | bytes 98312 | tf_op jit(solution)/shard_map/while/body/eval_jaxpr/ppermute | solution.py:21
  24.1 22.5 %collective-permute-start.1 = (bf16[128,1,128]{2,0,1:T(8,128)(2,1)S(1)}, bf16[128,1,128]{2,0,1:T(8,128)(2,1)S(1)}, u32[]{:S(2)}, u32[]{:S(2)}) collective-permute-start(bf16[128,1,128]{2,0,1:T(8,128)(2,1)S(1)} %copy.81), channel_id=1, source_target_pairs={{0,32},{32,64},{64,96},{96,128},{128,160},{160,192},{192,224},{224... | collective-permute-start | bytes 98312 | tf_op jit(solution)/shard_map/while/body/eval_jaxpr/ppermute | solution.py:21
  33.5 13.1 %collective-permute-start.2 = (s32[1]{0:T(128)}, s32[1]{0:T(128)}, u32[]{:S(2)}, u32[]{:S(2)}) collective-permute-start(s32[1]{0:T(128)} %copy.82), channel_id=1, source_target_pairs={{0,32},{32,64},{64,96},{96,128},{128,160},{160,192},{192,224},{224... | collective-permute-start | bytes 20 | tf_op jit(solution)/shard_map/while/body/eval_jaxpr/ppermute | solution.py:21
  54.8 24.8 %collective-permute-start = (bf16[128,1,128]{2,0,1:T(8,128)(2,1)S(1)}, bf16[128,1,128]{2,0,1:T(8,128)(2,1)S(1)}, u32[]{:S(2)}, u32[]{:S(2)}) collective-permute-start(bf16[128,1,128]{2,0,1:T(8,128)(2,1)S(1)} %copy.80), channel_id=1, source_target_pairs={{0,32},{32,64},{64,96},{96,128},{128,160},{160,192},{192,224},{224... | collective-permute-start | bytes 98312 | tf_op jit(solution)/shard_map/while/body/eval_jaxpr/ppermute | solution.py:21
  57.0 22.5 %collective-permute-start.1 = (bf16[128,1,128]{2,0,1:T(8,128)(2,1)S(1)}, bf16[128,1,128]{2,0,1:T(8,128)(2,1)S(1)}, u32[]{:S(2)}, u32[]{:S(2)}) collective-permute-start(bf16[128,1,128]{2,0,1:T(8,128)(2,1)S(1)} %copy.81), channel_id=1, source_target_pairs={{0,32},{32,64},{64,96},{96,128},{128,160},{160,192},{192,224},{224... | collective-permute-start | bytes 98312 | tf_op jit(solution)/shard_map/while/body/eval_jaxpr/ppermute | solution.py:21
  66.5 13.1 %collective-permute-start.2 = (s32[1]{0:T(128)}, s32[1]{0:T(128)}, u32[]{:S(2)}, u32[]{:S(2)}) collective-permute-start(s32[1]{0:T(128)} %copy.82), channel_id=1, source_target_pairs={{0,32},{32,64},{64,96},{96,128},{128,160},{160,192},{192,224},{224... | collective-permute-start | bytes 20 | tf_op jit(solution)/shard_map/while/body/eval_jaxpr/ppermute | solution.py:21
  88.4 23.7 %collective-permute-start = (bf16[128,1,128]{2,0,1:T(8,128)(2,1)S(1)}, bf16[128,1,128]{2,0,1:T(8,128)(2,1)S(1)}, u32[]{:S(2)}, u32[]{:S(2)}) collective-permute-start(bf16[128,1,128]{2,0,1:T(8,128)(2,1)S(1)} %copy.80), channel_id=1, source_target_pairs={{0,32},{32,64},{64,96},{96,128},{128,160},{160,192},{192,224},{224... | collective-permute-start | bytes 98312 | tf_op jit(solution)/shard_map/while/body/eval_jaxpr/ppermute | solution.py:21
  90.3 21.8 %collective-permute-start.1 = (bf16[128,1,128]{2,0,1:T(8,128)(2,1)S(1)}, bf16[128,1,128]{2,0,1:T(8,128)(2,1)S(1)}, u32[]{:S(2)}, u32[]{:S(2)}) collective-permute-start(bf16[128,1,128]{2,0,1:T(8,128)(2,1)S(1)} %copy.81), channel_id=1, source_target_pairs={{0,32},{32,64},{64,96},{96,128},{128,160},{160,192},{192,224},{224... | collective-permute-start | bytes 98312 | tf_op jit(solution)/shard_map/while/body/eval_jaxpr/ppermute | solution.py:21
  97.9 14.3 %collective-permute-start.2 = (s32[1]{0:T(128)}, s32[1]{0:T(128)}, u32[]{:S(2)}, u32[]{:S(2)}) collective-permute-start(s32[1]{0:T(128)} %copy.82), channel_id=1, source_target_pairs={{0,32},{32,64},{64,96},{96,128},{128,160},{160,192},{192,224},{224... | collective-permute-start | bytes 20 | tf_op jit(solution)/shard_map/while/body/eval_jaxpr/ppermute | solution.py:21
  120.9 23.0 %collective-permute-start = (bf16[128,1,128]{2,0,1:T(8,128)(2,1)S(1)}, bf16[128,1,128]{2,0,1:T(8,128)(2,1)S(1)}, u32[]{:S(2)}, u32[]{:S(2)}) collective-permute-start(bf16[128,1,128]{2,0,1:T(8,128)(2,1)S(1)} %copy.80), channel_id=1, source_target_pairs={{0,32},{32,64},{64,96},{96,128},{128,160},{160,192},{192,224},{224... | collective-permute-start | bytes 98312 | tf_op jit(solution)/shard_map/while/body/eval_jaxpr/ppermute | solution.py:21
  122.8 21.1 %collective-permute-start.1 = (bf16[128,1,128]{2,0,1:T(8,128)(2,1)S(1)}, bf16[128,1,128]{2,0,1:T(8,128)(2,1)S(1)}, u32[]{:S(2)}, u32[]{:S(2)}) collective-permute-start(bf16[128,1,128]{2,0,1:T(8,128)(2,1)S(1)} %copy.81), channel_id=1, source_target_pairs={{0,32},{32,64},{64,96},{96,128},{128,160},{160,192},{192,224},{224... | collective-permute-start | bytes 98312 | tf_op jit(solution)/shard_map/while/body/eval_jaxpr/ppermute | solution.py:21
  129.6 14.4 %collective-permute-start.2 = (s32[1]{0:T(128)}, s32[1]{0:T(128)}, u32[]{:S(2)}, u32[]{:S(2)}) collective-permute-start(s32[1]{0:T(128)} %copy.82), channel_id=1, source_target_pairs={{0,32},{32,64},{64,96},{96,128},{128,160},{160,192},{192,224},{224... | collective-permute-start | bytes 20 | tf_op jit(solution)/shard_map/while/body/eval_jaxpr/ppermute | solution.py:21
  141.7 13.1 %collective-permute-start.4 = (f32[128,1,128]{2,0,1:T(8,128)S(1)}, f32[128,1,128]{2,0,1:T(8,128)S(1)}, u32[]{:S(2)}, u32[]{:S(2)}) collective-permute-start(f32[128,1,128]{2,0,1:T(8,128)S(1)} %fusion.88), channel_id=1, source_target_pairs={{0,32},{32,64},{64,96},{96,128},{128,160},{160,192},{192,224},{224... | collective-permute-start | bytes 196616 | tf_op jit(solution)/shard_map/while/body/eval_jaxpr/ppermute | solution.py:21
  154.9 22.8 %collective-permute-start = (bf16[128,1,128]{2,0,1:T(8,128)(2,1)S(1)}, bf16[128,1,128]{2,0,1:T(8,128)(2,1)S(1)}, u32[]{:S(2)}, u32[]{:S(2)}) collective-permute-start(bf16[128,1,128]{2,0,1:T(8,128)(2,1)S(1)} %copy.80), channel_id=1, source_target_pairs={{0,32},{32,64},{64,96},{96,128},{128,160},{160,192},{192,224},{224... | collective-permute-start | bytes 98312 | tf_op jit(solution)/shard_map/while/body/eval_jaxpr/ppermute | solution.py:21
  156.8 20.9 %collective-permute-start.1 = (bf16[128,1,128]{2,0,1:T(8,128)(2,1)S(1)}, bf16[128,1,128]{2,0,1:T(8,128)(2,1)S(1)}, u32[]{:S(2)}, u32[]{:S(2)}) collective-permute-start(bf16[128,1,128]{2,0,1:T(8,128)(2,1)S(1)} %copy.81), channel_id=1, source_target_pairs={{0,32},{32,64},{64,96},{96,128},{128,160},{160,192},{192,224},{224... | collective-permute-start | bytes 98312 | tf_op jit(solution)/shard_map/while/body/eval_jaxpr/ppermute | solution.py:21
  159.9 17.8 %collective-permute-start.2 = (s32[1]{0:T(128)}, s32[1]{0:T(128)}, u32[]{:S(2)}, u32[]{:S(2)}) collective-permute-start(s32[1]{0:T(128)} %copy.82), channel_id=1, source_target_pairs={{0,32},{32,64},{64,96},{96,128},{128,160},{160,192},{192,224},{224... | collective-permute-start | bytes 20 | tf_op jit(solution)/shard_map/while/body/eval_jaxpr/ppermute | solution.py:21
  186.5 23.9 %collective-permute-start = (bf16[128,1,128]{2,0,1:T(8,128)(2,1)S(1)}, bf16[128,1,128]{2,0,1:T(8,128)(2,1)S(1)}, u32[]{:S(2)}, u32[]{:S(2)}) collective-permute-start(bf16[128,1,128]{2,0,1:T(8,128)(2,1)S(1)} %copy.80), channel_id=1, source_target_pairs={{0,32},{32,64},{64,96},{96,128},{128,160},{160,192},{192,224},{224... | collective-permute-start | bytes 98312 | tf_op jit(solution)/shard_map/while/body/eval_jaxpr/ppermute | solution.py:21
  188.5 21.9 %collective-permute-start.1 = (bf16[128,1,128]{2,0,1:T(8,128)(2,1)S(1)}, bf16[128,1,128]{2,0,1:T(8,128)(2,1)S(1)}, u32[]{:S(2)}, u32[]{:S(2)}) collective-permute-start(bf16[128,1,128]{2,0,1:T(8,128)(2,1)S(1)} %copy.81), channel_id=1, source_target_pairs={{0,32},{32,64},{64,96},{96,128},{128,160},{160,192},{192,224},{224... | collective-permute-start | bytes 98312 | tf_op jit(solution)/shard_map/while/body/eval_jaxpr/ppermute | solution.py:21
  194.7 15.7 %collective-permute-start.2 = (s32[1]{0:T(128)}, s32[1]{0:T(128)}, u32[]{:S(2)}, u32[]{:S(2)}) collective-permute-start(s32[1]{0:T(128)} %copy.82), channel_id=1, source_target_pairs={{0,32},{32,64},{64,96},{96,128},{128,160},{160,192},{192,224},{224... | collective-permute-start | bytes 20 | tf_op jit(solution)/shard_map/while/body/eval_jaxpr/ppermute | solution.py:21
  208.1 14.4 %collective-permute-start.4 = (f32[128,1,128]{2,0,1:T(8,128)S(1)}, f32[128,1,128]{2,0,1:T(8,128)S(1)}, u32[]{:S(2)}, u32[]{:S(2)}) collective-permute-start(f32[128,1,128]{2,0,1:T(8,128)S(1)} %fusion.88), channel_id=1, source_target_pairs={{0,32},{32,64},{64,96},{96,128},{128,160},{160,192},{192,224},{224... | collective-permute-start | bytes 196616 | tf_op jit(solution)/shard_map/while/body/eval_jaxpr/ppermute | solution.py:21
  222.6 21.4 %collective-permute-start = (bf16[128,1,128]{2,0,1:T(8,128)(2,1)S(1)}, bf16[128,1,128]{2,0,1:T(8,128)(2,1)S(1)}, u32[]{:S(2)}, u32[]{:S(2)}) collective-permute-start(bf16[128,1,128]{2,0,1:T(8,128)(2,1)S(1)} %copy.80), channel_id=1, source_target_pairs={{0,32},{32,64},{64,96},{96,128},{128,160},{160,192},{192,224},{224... | collective-permute-start | bytes 98312 | tf_op jit(solution)/shard_map/while/body/eval_jaxpr/ppermute | solution.py:21
  224.5 19.5 %collective-permute-start.1 = (bf16[128,1,128]{2,0,1:T(8,128)(2,1)S(1)}, bf16[128,1,128]{2,0,1:T(8,128)(2,1)S(1)}, u32[]{:S(2)}, u32[]{:S(2)}) collective-permute-start(bf16[128,1,128]{2,0,1:T(8,128)(2,1)S(1)} %copy.81), channel_id=1, source_target_pairs={{0,32},{32,64},{64,96},{96,128},{128,160},{160,192},{192,224},{224... | collective-permute-start | bytes 98312 | tf_op jit(solution)/shard_map/while/body/eval_jaxpr/ppermute | solution.py:21
  227.0 17.0 %collective-permute-start.2 = (s32[1]{0:T(128)}, s32[1]{0:T(128)}, u32[]{:S(2)}, u32[]{:S(2)}) collective-permute-start(s32[1]{0:T(128)} %copy.82), channel_id=1, source_target_pairs={{0,32},{32,64},{64,96},{96,128},{128,160},{160,192},{192,224},{224... | collective-permute-start | bytes 20 | tf_op jit(solution)/shard_map/while/body/eval_jaxpr/ppermute | solution.py:21
  252.8 28.1 %collective-permute-start = (bf16[128,1,128]{2,0,1:T(8,128)(2,1)S(1)}, bf16[128,1,128]{2,0,1:T(8,128)(2,1)S(1)}, u32[]{:S(2)}, u32[]{:S(2)}) collective-permute-start(bf16[128,1,128]{2,0,1:T(8,128)(2,1)S(1)} %copy.80), channel_id=1, source_target_pairs={{0,32},{32,64},{64,96},{96,128},{128,160},{160,192},{192,224},{224... | collective-permute-start | bytes 98312 | tf_op jit(solution)/shard_map/while/body/eval_jaxpr/ppermute | solution.py:21
  254.7 26.2 %collective-permute-start.1 = (bf16[128,1,128]{2,0,1:T(8,128)(2,1)S(1)}, bf16[128,1,128]{2,0,1:T(8,128)(2,1)S(1)}, u32[]{:S(2)}, u32[]{:S(2)}) collective-permute-start(bf16[128,1,128]{2,0,1:T(8,128)(2,1)S(1)} %copy.81), channel_id=1, source_target_pairs={{0,32},{32,64},{64,96},{96,128},{128,160},{160,192},{192,224},{224... | collective-permute-start | bytes 98312 | tf_op jit(solution)/shard_map/while/body/eval_jaxpr/ppermute | solution.py:21
  257.2 23.6 %collective-permute-start.2 = (s32[1]{0:T(128)}, s32[1]{0:T(128)}, u32[]{:S(2)}, u32[]{:S(2)}) collective-permute-start(s32[1]{0:T(128)} %copy.82), channel_id=1, source_target_pairs={{0,32},{32,64},{64,96},{96,128},{128,160},{160,192},{192,224},{224... | collective-permute-start | bytes 20 | tf_op jit(solution)/shard_map/while/body/eval_jaxpr/ppermute | solution.py:21
  278.6 15.4 %collective-permute-start.4 = (f32[128,1,128]{2,0,1:T(8,128)S(1)}, f32[128,1,128]{2,0,1:T(8,128)S(1)}, u32[]{:S(2)}, u32[]{:S(2)}) collective-permute-start(f32[128,1,128]{2,0,1:T(8,128)S(1)} %fusion.88), channel_id=1, source_target_pairs={{0,32},{32,64},{64,96},{96,128},{128,160},{160,192},{192,224},{224... | collective-permute-start | bytes 196616 | tf_op jit(solution)/shard_map/while/body/eval_jaxpr/ppermute | solution.py:21
  294.0 15.1 %collective-permute-start = (bf16[128,1,128]{2,0,1:T(8,128)(2,1)S(1)}, bf16[128,1,128]{2,0,1:T(8,128)(2,1)S(1)}, u32[]{:S(2)}, u32[]{:S(2)}) collective-permute-start(bf16[128,1,128]{2,0,1:T(8,128)(2,1)S(1)} %copy.80), channel_id=1, source_target_pairs={{0,32},{32,64},{64,96},{96,128},{128,160},{160,192},{192,224},{224... | collective-permute-start | bytes 98312 | tf_op jit(solution)/shard_map/while/body/eval_jaxpr/ppermute | solution.py:21
  296.0 13.2 %collective-permute-start.1 = (bf16[128,1,128]{2,0,1:T(8,128)(2,1)S(1)}, bf16[128,1,128]{2,0,1:T(8,128)(2,1)S(1)}, u32[]{:S(2)}, u32[]{:S(2)}) collective-permute-start(bf16[128,1,128]{2,0,1:T(8,128)(2,1)S(1)} %copy.81), channel_id=1, source_target_pairs={{0,32},{32,64},{64,96},{96,128},{128,160},{160,192},{192,224},{224... | collective-permute-start | bytes 98312 | tf_op jit(solution)/shard_map/while/body/eval_jaxpr/ppermute | solution.py:21
  318.2 30.3 %collective-permute-start = (bf16[128,1,128]{2,0,1:T(8,128)(2,1)S(1)}, bf16[128,1,128]{2,0,1:T(8,128)(2,1)S(1)}, u32[]{:S(2)}, u32[]{:S(2)}) collective-permute-start(bf16[128,1,128]{2,0,1:T(8,128)(2,1)S(1)} %copy.80), channel_id=1, source_target_pairs={{0,32},{32,64},{64,96},{96,128},{128,160},{160,192},{192,224},{224... | collective-permute-start | bytes 98312 | tf_op jit(solution)/shard_map/while/body/eval_jaxpr/ppermute | solution.py:21
  320.1 28.4 %collective-permute-start.1 = (bf16[128,1,128]{2,0,1:T(8,128)(2,1)S(1)}, bf16[128,1,128]{2,0,1:T(8,128)(2,1)S(1)}, u32[]{:S(2)}, u32[]{:S(2)}) collective-permute-start(bf16[128,1,128]{2,0,1:T(8,128)(2,1)S(1)} %copy.81), channel_id=1, source_target_pairs={{0,32},{32,64},{64,96},{96,128},{128,160},{160,192},{192,224},{224... | collective-permute-start | bytes 98312 | tf_op jit(solution)/shard_map/while/body/eval_jaxpr/ppermute | solution.py:21
  323.0 25.5 %collective-permute-start.2 = (s32[1]{0:T(128)}, s32[1]{0:T(128)}, u32[]{:S(2)}, u32[]{:S(2)}) collective-permute-start(s32[1]{0:T(128)} %copy.82), channel_id=1, source_target_pairs={{0,32},{32,64},{64,96},{96,128},{128,160},{160,192},{192,224},{224... | collective-permute-start | bytes 20 | tf_op jit(solution)/shard_map/while/body/eval_jaxpr/ppermute | solution.py:21
  356.5 16.7 %collective-permute-start = (bf16[128,1,128]{2,0,1:T(8,128)(2,1)S(1)}, bf16[128,1,128]{2,0,1:T(8,128)(2,1)S(1)}, u32[]{:S(2)}, u32[]{:S(2)}) collective-permute-start(bf16[128,1,128]{2,0,1:T(8,128)(2,1)S(1)} %copy.80), channel_id=1, source_target_pairs={{0,32},{32,64},{64,96},{96,128},{128,160},{160,192},{192,224},{224... | collective-permute-start | bytes 98312 | tf_op jit(solution)/shard_map/while/body/eval_jaxpr/ppermute | solution.py:21
  358.4 14.8 %collective-permute-start.1 = (bf16[128,1,128]{2,0,1:T(8,128)(2,1)S(1)}, bf16[128,1,128]{2,0,1:T(8,128)(2,1)S(1)}, u32[]{:S(2)}, u32[]{:S(2)}) collective-permute-start(bf16[128,1,128]{2,0,1:T(8,128)(2,1)S(1)} %copy.81), channel_id=1, source_target_pairs={{0,32},{32,64},{64,96},{96,128},{128,160},{160,192},{192,224},{224... | collective-permute-start | bytes 98312 | tf_op jit(solution)/shard_map/while/body/eval_jaxpr/ppermute | solution.py:21
  382.6 36.0 %collective-permute-start = (bf16[128,1,128]{2,0,1:T(8,128)(2,1)S(1)}, bf16[128,1,128]{2,0,1:T(8,128)(2,1)S(1)}, u32[]{:S(2)}, u32[]{:S(2)}) collective-permute-start(bf16[128,1,128]{2,0,1:T(8,128)(2,1)S(1)} %copy.80), channel_id=1, source_target_pairs={{0,32},{32,64},{64,96},{96,128},{128,160},{160,192},{192,224},{224... | collective-permute-start | bytes 98312 | tf_op jit(solution)/shard_map/while/body/eval_jaxpr/ppermute | solution.py:21
  384.5 34.1 %collective-permute-start.1 = (bf16[128,1,128]{2,0,1:T(8,128)(2,1)S(1)}, bf16[128,1,128]{2,0,1:T(8,128)(2,1)S(1)}, u32[]{:S(2)}, u32[]{:S(2)}) collective-permute-start(bf16[128,1,128]{2,0,1:T(8,128)(2,1)S(1)} %copy.81), channel_id=1, source_target_pairs={{0,32},{32,64},{64,96},{96,128},{128,160},{160,192},{192,224},{224... | collective-permute-start | bytes 98312 | tf_op jit(solution)/shard_map/while/body/eval_jaxpr/ppermute | solution.py:21
  395.4 23.2 %collective-permute-start.2 = (s32[1]{0:T(128)}, s32[1]{0:T(128)}, u32[]{:S(2)}, u32[]{:S(2)}) collective-permute-start(s32[1]{0:T(128)} %copy.82), channel_id=1, source_target_pairs={{0,32},{32,64},{64,96},{96,128},{128,160},{160,192},{192,224},{224... | collective-permute-start | bytes 20 | tf_op jit(solution)/shard_map/while/body/eval_jaxpr/ppermute | solution.py:21
  429.4 15.1 %collective-permute-start = (bf16[128,1,128]{2,0,1:T(8,128)(2,1)S(1)}, bf16[128,1,128]{2,0,1:T(8,128)(2,1)S(1)}, u32[]{:S(2)}, u32[]{:S(2)}) collective-permute-start(bf16[128,1,128]{2,0,1:T(8,128)(2,1)S(1)} %copy.80), channel_id=1, source_target_pairs={{0,32},{32,64},{64,96},{96,128},{128,160},{160,192},{192,224},{224... | collective-permute-start | bytes 98312 | tf_op jit(solution)/shard_map/while/body/eval_jaxpr/ppermute | solution.py:21
  431.3 13.1 %collective-permute-start.1 = (bf16[128,1,128]{2,0,1:T(8,128)(2,1)S(1)}, bf16[128,1,128]{2,0,1:T(8,128)(2,1)S(1)}, u32[]{:S(2)}, u32[]{:S(2)}) collective-permute-start(bf16[128,1,128]{2,0,1:T(8,128)(2,1)S(1)} %copy.81), channel_id=1, source_target_pairs={{0,32},{32,64},{64,96},{96,128},{128,160},{160,192},{192,224},{224... | collective-permute-start | bytes 98312 | tf_op jit(solution)/shard_map/while/body/eval_jaxpr/ppermute | solution.py:21
  451.9 25.2 %collective-permute-start = (bf16[128,1,128]{2,0,1:T(8,128)(2,1)S(1)}, bf16[128,1,128]{2,0,1:T(8,128)(2,1)S(1)}, u32[]{:S(2)}, u32[]{:S(2)}) collective-permute-start(bf16[128,1,128]{2,0,1:T(8,128)(2,1)S(1)} %copy.80), channel_id=1, source_target_pairs={{0,32},{32,64},{64,96},{96,128},{128,160},{160,192},{192,224},{224... | collective-permute-start | bytes 98312 | tf_op jit(solution)/shard_map/while/body/eval_jaxpr/ppermute | solution.py:21
  453.8 23.3 %collective-permute-start.1 = (bf16[128,1,128]{2,0,1:T(8,128)(2,1)S(1)}, bf16[128,1,128]{2,0,1:T(8,128)(2,1)S(1)}, u32[]{:S(2)}, u32[]{:S(2)}) collective-permute-start(bf16[128,1,128]{2,0,1:T(8,128)(2,1)S(1)} %copy.81), channel_id=1, source_target_pairs={{0,32},{32,64},{64,96},{96,128},{128,160},{160,192},{192,224},{224... | collective-permute-start | bytes 98312 | tf_op jit(solution)/shard_map/while/body/eval_jaxpr/ppermute | solution.py:21
  457.2 19.8 %collective-permute-start.2 = (s32[1]{0:T(128)}, s32[1]{0:T(128)}, u32[]{:S(2)}, u32[]{:S(2)}) collective-permute-start(s32[1]{0:T(128)} %copy.82), channel_id=1, source_target_pairs={{0,32},{32,64},{64,96},{96,128},{128,160},{160,192},{192,224},{224... | collective-permute-start | bytes 20 | tf_op jit(solution)/shard_map/while/body/eval_jaxpr/ppermute | solution.py:21
  486.9 22.7 %collective-permute-start = (bf16[128,1,128]{2,0,1:T(8,128)(2,1)S(1)}, bf16[128,1,128]{2,0,1:T(8,128)(2,1)S(1)}, u32[]{:S(2)}, u32[]{:S(2)}) collective-permute-start(bf16[128,1,128]{2,0,1:T(8,128)(2,1)S(1)} %copy.80), channel_id=1, source_target_pairs={{0,32},{32,64},{64,96},{96,128},{128,160},{160,192},{192,224},{224... | collective-permute-start | bytes 98312 | tf_op jit(solution)/shard_map/while/body/eval_jaxpr/ppermute | solution.py:21
  488.8 20.8 %collective-permute-start.1 = (bf16[128,1,128]{2,0,1:T(8,128)(2,1)S(1)}, bf16[128,1,128]{2,0,1:T(8,128)(2,1)S(1)}, u32[]{:S(2)}, u32[]{:S(2)}) collective-permute-start(bf16[128,1,128]{2,0,1:T(8,128)(2,1)S(1)} %copy.81), channel_id=1, source_target_pairs={{0,32},{32,64},{64,96},{96,128},{128,160},{160,192},{192,224},{224... | collective-permute-start | bytes 98312 | tf_op jit(solution)/shard_map/while/body/eval_jaxpr/ppermute | solution.py:21
  491.3 18.3 %collective-permute-start.2 = (s32[1]{0:T(128)}, s32[1]{0:T(128)}, u32[]{:S(2)}, u32[]{:S(2)}) collective-permute-start(s32[1]{0:T(128)} %copy.82), channel_id=1, source_target_pairs={{0,32},{32,64},{64,96},{96,128},{128,160},{160,192},{192,224},{224... | collective-permute-start | bytes 20 | tf_op jit(solution)/shard_map/while/body/eval_jaxpr/ppermute | solution.py:21
  495.3 14.3 %collective-permute-start.3 = (f32[128,1,128]{2,0,1:T(8,128)S(1)}, f32[128,1,128]{2,0,1:T(8,128)S(1)}, u32[]{:S(2)}, u32[]{:S(2)}) collective-permute-start(f32[128,1,128]{2,0,1:T(8,128)S(1)} %fusion.87), channel_id=1, source_target_pairs={{0,32},{32,64},{64,96},{96,128},{128,160},{160,192},{192,224},{224... | collective-permute-start | bytes 196616 | tf_op jit(solution)/shard_map/while/body/eval_jaxpr/ppermute | solution.py:21
  528.6 214.0 %all-gather.4.cloned.1.call-start = ((), (), s32[]{:S(2)}) async-start(), calls=%async_computation | async-start | bytes 2785280 | tf_op jit(solution)/shard_map/all_gather | solution.py:13
  (34 other events, 993.4 us)
Sparse Core Ops, SparseCore 0:
  528.7 106.6 all-gather.5
  639.0 103.5 all-gather.3
